TPU v7x, 512 devices: a whole 4x4x16 slice. The times are simulated.
512 devices in a mesh: expert: 64 (over y, z), tensor: 8 (over x, core).
Axes of the slice: x: 4, y: 4, z: 16, core: 2. Of those that a mesh axis runs over, the one named last changes fastest.
Arguments:
- tokens: bfloat16 [65536, 1024], P(('expert', 'tensor')), may hold values from -6 to 6
- out_grad: bfloat16 [65536, 1024], P(('expert', 'tensor')), may hold values from -6 to 6
- expert_ids: int32 [65536, 2], P(('expert', 'tensor')), may hold values from 0 to 63, all different within a row; in each aligned block of 128 rows (0 to 127, 128 to 255, ...) at most 5 rows name the same one
- gate_levels: int32 [65536, 2], P(('expert', 'tensor')), may hold values from 1 to 255
- gate_weight: bfloat16 [64, 1024, 2048], P('expert', None, 'tensor'), may hold values from -0.1875 to 0.1875
- up_weight: bfloat16 [64, 1024, 2048], P('expert', None, 'tensor'), may hold values from -0.1875 to 0.1875
- down_weight: bfloat16 [64, 1024, 2048], P('expert', None, 'tensor'), may hold values from -0.125 to 0.125
Outputs:
- token_grad: bfloat16 [65536, 1024], P(('expert', 'tensor'))
Inputs may be any that keep to these rules, and one draw needn't show every extreme that they name: `expert_ids`: A token's 2 experts differ. Among the 128 tokens of one device no expert is named more than 5 times, a bound that some block reaches.
All inputs are finite; a program needn't handle non-finite values.
Results may differ from a plain program's by a relative error of at most 0.01.
Values may be sent and summed in bfloat16 or wider, within the bound.
No kernel may reach another device: no remote copies, remote signals or barrier semaphores. Data moves between devices by JAX's collectives and lax.ppermute only.
A program may use at most 64 MiB of HBM per device.

v0:
```python
import jax
import jax.numpy as jnp
from jax import lax
from jax.sharding import PartitionSpec as P

level_scale = 1.0 / 256.0


def expert_grad(rows_in, grads_in, gate_cols, up_cols, down_cols):
    gate_pre = jnp.dot(rows_in, gate_cols, preferred_element_type=jnp.float32)
    up_pre = jnp.dot(rows_in, up_cols, preferred_element_type=jnp.float32)
    hidden_grad = jnp.dot(grads_in, down_cols, preferred_element_type=jnp.float32)
    sigmoid_val = jax.nn.sigmoid(gate_pre)
    up_grad = (hidden_grad * gate_pre * sigmoid_val).astype(jnp.bfloat16)
    gate_grad = (
        hidden_grad * up_pre * sigmoid_val * (1.0 + gate_pre * (1.0 - sigmoid_val))
    ).astype(jnp.bfloat16)
    joined_grad = jnp.concatenate([gate_grad, up_grad], axis=1)
    joined_cols = jnp.concatenate([gate_cols, up_cols], axis=1)
    back_dims = (((1,), (1,)), ((), ()))
    result = lax.dot_general(
        joined_grad, joined_cols, back_dims, preferred_element_type=jnp.float32
    )
    return result.astype(jnp.bfloat16)


def on_device(tokens, out_grad, expert_ids, gate_levels, gate_weight, up_weight, down_weight):
    tok_count, width = tokens.shape
    top_count = expert_ids.shape[1]
    experts = lax.axis_size("expert")
    capacity = max(2, 5 * tok_count * top_count // (4 * experts))
    slots = experts * capacity
    flat_ids = expert_ids.reshape(-1)
    lane_ids = jnp.arange(experts, dtype=jnp.int32)
    onehot = (flat_ids[:, None] == lane_ids[None, :]).astype(jnp.int32)
    slot_rank = jnp.sum(jnp.cumsum(onehot, axis=0) * onehot, axis=1) - 1
    slot_ids = flat_ids * capacity + slot_rank
    assign = (slot_ids[:, None] == jnp.arange(slots, dtype=jnp.int32)[None, :]).astype(jnp.float32)
    assign = assign.reshape(tok_count, top_count, slots)
    dispatch = jnp.sum(assign, axis=1).astype(jnp.bfloat16)
    route_scale = gate_levels.astype(jnp.float32) * level_scale
    combiner = jnp.sum(assign * route_scale[:, :, None], axis=1)
    send_dims = (((0,), (0,)), ((), ()))
    send_rows = lax.dot_general(
        dispatch, tokens, send_dims, preferred_element_type=jnp.float32
    ).astype(jnp.bfloat16)
    send_grads = lax.dot_general(
        dispatch, out_grad, send_dims, preferred_element_type=jnp.float32
    ).astype(jnp.bfloat16)
    packed = jnp.stack([send_rows, send_grads])
    received = lax.all_to_all(packed, "expert", split_axis=1, concat_axis=1, tiled=True)
    gate_cols = gate_weight[0]
    up_cols = up_weight[0]
    down_cols = down_weight[0]
    part_rows = lax.all_gather(received, "tensor", axis=1, tiled=True)
    partials = expert_grad(part_rows[0], part_rows[1], gate_cols, up_cols, down_cols)
    partials = partials.reshape(-1, slots, width)
    returned = lax.all_to_all(
        lax.all_to_all(partials, "expert", split_axis=1, concat_axis=1, tiled=True),
        "tensor",
        split_axis=0,
        concat_axis=0,
        tiled=True,
    )
    contrib = jnp.sum(returned.astype(jnp.float32), axis=0)
    token_grad = jnp.dot(
        combiner, contrib, precision=lax.Precision.HIGHEST, preferred_element_type=jnp.float32
    )
    return token_grad.astype(jnp.bfloat16)


def solution(mesh):
    return jax.shard_map(
        on_device,
        mesh=mesh,
        in_specs=(
            P(("expert", "tensor"), None),
            P(("expert", "tensor"), None),
            P(("expert", "tensor"), None),
            P(("expert", "tensor"), None),
            P("expert", None, "tensor"),
            P("expert", None, "tensor"),
            P("expert", None, "tensor"),
        ),
        out_specs=P(("expert", "tensor"), None),
        check_vma=False,
    )
```

profile of v0, /device:TPU:1, one launch (start us, length us, event | category | flops | bytes accessed | tf_op | source)
XLA Modules:
  0.0 501.7 jit_solution(4049381263710705938)
XLA Ops:
  6.5 0.0 copy-start
  6.5 0.0 all-gather.2.cloned.1.call-start
  6.5 0.8 copy.53
  7.4 0.1 eq.39
  7.5 0.1 eq.43
  7.7 0.6 reduce-window.6
  8.3 0.2 slice_reduce_fusion
  8.5 0.1 fusion.17
  8.6 0.1 sub.10
  8.8 0.1 copy.56
  8.8 0.7 multiply_add_fusion
  9.6 0.7 convert_multiply_fusion
  10.2 0.1 convert_reduce_fusion.1
  10.3 1.3 fusion.11
  11.6 1.3 fusion.10
  12.9 0.1 pad_maximum_fusion
  13.0 1.3 copy.57
  14.3 79.5 %all_to_all.15 = bf16[2,320,1024]{2,0,1:T(2,128)(2,1)S(1)} all-to-all(bf16[2,320,1024]{2,0,1:T(2,128)(2,1)S(1)} %copy.57), channel_id=1, replica_groups=mesh['expert'=64,'tensor'=8] {'expert'}, dimensions={1} | all-to-all | bytes 2621440 | tf_op jit(solution)/shard_map/all_to_all | solution.py:51
  93.9 0.0 copy-start.2
  93.9 1.4 copy.58
  95.3 0.0 all-gather.2.cloned.1.call-update
  95.3 64.1 %all-gather.2.cloned.1.call-done = bf16[2,2560,1024]{2,1,0:T(8,128)(2,1)} async-done(((bf16[2,320,1024]{2,1,0:T(8,128)(2,1)}), bf16[2,2560,1024]{2,1,0:T(8,128)(2,1)}) %all-gather.2.cloned.1.call-update) | async-done | bytes 10485776 | tf_op jit(solution)/shard_map/all_gather | solution.py:55
  159.4 0.0 copy-done.2
  159.5 0.0 copy-start.1
  159.5 4.2 fusion.1
  163.7 0.0 copy-done
  163.7 1.3 copy-done.1
  165.0 0.0 copy-start.3
  165.0 2.2 multiply_convert_fusion
  167.2 0.0 copy-done.3
  167.2 2.6 fusion.6
  169.7 3.2 convolution_convert_fusion
  173.0 2.9 copy.59
  175.9 245.5 %all_to_all.16 = bf16[8,320,1024]{2,0,1:T(8,128)(2,1)S(1)} all-to-all(bf16[8,320,1024]{2,0,1:T(8,128)(2,1)S(1)} %copy.59), channel_id=1, replica_groups=mesh['expert'=64,'tensor'=8] {'expert'}, dimensions={1} | all-to-all | bytes 10485760 | tf_op jit(solution)/shard_map/all_to_all | solution.py:59
  421.3 2.9 copy.60
  424.2 67.6 %all_to_all.17 = bf16[8,320,1024]{2,1,0:T(8,128)(2,1)S(1)} all-to-all(bf16[8,320,1024]{2,1,0:T(8,128)(2,1)S(1)} %copy.60), channel_id=1, replica_groups=mesh['expert'=64,'tensor'=8] {'tensor'}, dimensions={0} | all-to-all | bytes 10485760 | tf_op jit(solution)/shard_map/all_to_all | solution.py:58
  491.9 1.2 convert_reduce_fusion
  493.0 1.8 convolution_convert_fusion.3
  (4 shorter events, 0.1 us)
Async XLA Ops:
  6.5 157.2 %copy-start = (bf16[1,1024,256]{2,1,0:T(8,128)(2,1)S(1)}, bf16[1,1024,256]{2,1,0:T(8,128)(2,1)}, u32[]{:S(2)}) copy-start(bf16[1,1024,256]{2,1,0:T(8,128)(2,1)} %param.13) | copy-start | bytes 1572868
  6.5 152.9 %all-gather.2.cloned.1.call-start = ((), (), s32[]{:S(2)}) async-start(), calls=%async_computation.3 | async-start | bytes 11796480 | tf_op jit(solution)/shard_map/all_gather | solution.py:55
  93.9 65.6 %copy-start.2 = (bf16[1,1024,256]{2,1,0:T(8,128)(2,1)S(1)}, bf16[1,1024,256]{2,1,0:T(8,128)(2,1)}, u32[]{:S(2)}) copy-start(bf16[1,1024,256]{2,1,0:T(8,128)(2,1)} %param.11) | copy-start | bytes 1572868
  159.5 5.5 %copy-start.1 = (bf16[2,2560,1024]{2,1,0:T(8,128)(2,1)S(1)}, bf16[2,2560,1024]{2,1,0:T(8,128)(2,1)}, u32[]{:S(2)}) copy-start(bf16[2,2560,1024]{2,1,0:T(8,128)(2,1)} %all-gather.2.cloned.1.call-done) | copy-start | bytes 31457284
  165.0 2.2 copy-start.3
Sparse Core Ops, SparseCore 0:
  95.4 63.9 all-gather.1
where the time goes:
time: 502 us
  blocking collectives  393 us (78%)
  waiting for transfers between devices  64.2 us (13%)
  matrix products  16.5 us (3%)
  between operations  13.5 us (3%)
  local copies, waits for them, and re-layouts  11.4 us (2%)
    all_to_all x1, blocking collectives, on_device(): lax.all_to_all(partials, 'expert', split_axis=1, concat_axis=1, tiled=True)  245 us
    all_to_all x1, blocking collectives, on_device(): lax.all_to_all(packed, 'expert', split_axis=1, concat_axis=1, tiled=True)  79.5 us
    all_to_all x1, blocking collectives, on_device(): lax.all_to_all(lax.all_to_all(partials, 'expert', split_axis=1, concat_ax...  67.6 us
    all_gather x1, waiting for transfers between devices, on_device(): part_rows = lax.all_gather(received, 'tensor', axis=1, tiled=True)  64.1 us
  transfers between devices with their start and end apart: 1, of which 1 were waited for; matrix products, arithmetic and copies ran while one was open for 0% of the time, Pallas kernels for 0%

commit v1 on v0

--- a/solution.py
+++ b/solution.py
@@ -52,7 +52,9 @@
     gate_cols = gate_weight[0]
     up_cols = up_weight[0]
     down_cols = down_weight[0]
-    part_rows = lax.all_gather(received, "tensor", axis=1, tiled=True)
+    part_rows = jnp.concatenate(
+        lax.all_to_all(jnp.stack([received] * lax.axis_size("tensor")), "tensor", 0, 0), axis=1
+    )
     partials = expert_grad(part_rows[0], part_rows[1], gate_cols, up_cols, down_cols)
     partials = partials.reshape(-1, slots, width)
     returned = lax.all_to_all(

time: 502 us -> 556 us (1.11)
  blocking collectives: 393 us -> 512 us
  waiting for transfers between devices: 64.2 us -> 0 us
  between operations: 13.5 us -> 0.2 us
  local copies, waits for them, and re-layouts: 11.4 us -> 23.9 us
    all_to_all x0 -> x1, blocking collectives: none -> 128 us  [on_device(): lax.all_to_all(jnp.stack([received] * lax.axis_size('tensor')), 'tensor',...]
    all_gather x1 -> x0, waiting for transfers between devices: 64.1 us -> none  [on_device(): part_rows = lax.all_gather(received, 'tensor', axis=1, tiled=True)]
    slice x1 -> x2, local copies, waits for them, and re-layouts: 0.18 us -> 9.84 us  [the longest x1 9.65 us: on_device(): part_rows[0]]
    all_to_all x1, blocking collectives: 245 us -> 236 us  [on_device(): lax.all_to_all(partials, 'expert', split_axis=1, concat_axis=1, tiled=True)]
  transfers between devices with their start and end apart: 1 -> 0, of which waited for: 1 -> 0; matrix products, arithmetic and copies ran while one was open for 0% -> 0% of each run, Pallas kernels for 0% -> 0%
where the time goes in v1:
time: 556 us
  blocking collectives  512 us (92%)
  local copies, waits for them, and re-layouts  23.9 us (4%)
  matrix products  16.3 us (3%)
    all_to_all x1, blocking collectives, on_device(): lax.all_to_all(partials, 'expert', split_axis=1, concat_axis=1, tiled=True)  236 us
    all_to_all x1, blocking collectives, on_device(): lax.all_to_all(jnp.stack([received] * lax.axis_size('tensor')), 'tensor',...  128 us
    all_to_all x1, blocking collectives, on_device(): lax.all_to_all(packed, 'expert', split_axis=1, concat_axis=1, tiled=True)  79.6 us
    all_to_all x1, blocking collectives, on_device(): lax.all_to_all(lax.all_to_all(partials, 'expert', split_axis=1, concat_ax...  68.3 us

profile of v1, /device:TPU:1, one launch (start us, length us, event | category | flops | bytes accessed | tf_op | source)
XLA Modules:
  0.0 555.6 jit_solution(605586059623427668)
XLA Ops:
  0.0 0.0 copy-start
  0.0 0.8 copy.45
  0.8 0.1 eq.43
  1.0 0.1 eq.39
  1.1 0.7 convert_multiply_fusion
  1.8 0.6 reduce-window.6
  2.4 0.2 slice_reduce_fusion
  2.7 0.1 fusion.14
  2.8 0.1 sub.10
  2.9 0.1 copy.48
  3.0 0.7 multiply_add_fusion
  3.7 0.1 convert_reduce_fusion.1
  3.8 1.3 fusion.7
  5.0 1.3 fusion.6
  6.3 0.1 pad_maximum_fusion
  6.5 1.3 copy.49
  7.8 79.6 %all_to_all.20 = bf16[2,320,1024]{2,0,1:T(2,128)(2,1)S(1)} all-to-all(bf16[2,320,1024]{2,0,1:T(2,128)(2,1)S(1)} %copy.49), channel_id=1, replica_groups=mesh['expert'=64,'tensor'=8] {'expert'}, dimensions={1} | all-to-all | bytes 2621440 | tf_op jit(solution)/shard_map/all_to_all | solution.py:51
  87.4 0.3 copy.50
  87.7 5.2 stack.11
  93.0 127.8 %all_to_all.21 = bf16[8,2,320,1024]{3,2,1,0:T(8,128)(2,1)} all-to-all(bf16[8,2,320,1024]{3,2,1,0:T(8,128)(2,1)} %stack.11), channel_id=1, replica_groups=mesh['expert'=64,'tensor'=8] {'tensor'}, dimensions={0} | all-to-all | bytes 20971520 | tf_op jit(solution)/shard_map/all_to_all | solution.py:56
  220.7 0.0 copy-start.3
  220.8 9.7 %fusion.22 = (bf16[1,8,320,1024]{3,2,0,1:T(8,128)(2,1)}, bf16[1,8,320,1024]{3,2,0,1:T(8,128)(2,1)}) fusion(bf16[2,8,320,1024]{3,2,0,1:T(8,128)(2,1)} %bitcast.43), kind=kLoop, calls=%fused_computation.42 | loop fusion | bytes 20971520 | tf_op jit(solution)/shard_map/slice | solution.py:58
  230.4 0.0 copy-done.3
  230.4 0.0 copy-start.2
  230.4 0.0 slice-start
  230.4 4.2 fusion.19
  234.7 0.0 copy-done
  234.7 0.0 copy-done.2
  234.7 0.0 slice-start.1
  234.7 0.0 copy-start.4
  234.7 2.1 multiply_convert_fusion
  236.8 0.0 slice-done
  236.8 0.0 slice-done.1
  236.8 0.0 copy-done.4
  236.8 2.5 fusion.2
  239.3 3.2 convolution_convert_fusion
  242.5 2.9 copy.51
  245.4 236.1 %all_to_all.22 = bf16[8,320,1024]{2,0,1:T(8,128)(2,1)S(1)} all-to-all(bf16[8,320,1024]{2,0,1:T(8,128)(2,1)S(1)} %copy.51), channel_id=1, replica_groups=mesh['expert'=64,'tensor'=8] {'expert'}, dimensions={1} | all-to-all | bytes 10485760 | tf_op jit(solution)/shard_map/all_to_all | solution.py:61
  481.5 2.9 copy.52
  484.4 0.0 copy-start.1
  484.4 68.3 %all_to_all.23 = bf16[8,320,1024]{2,1,0:T(8,128)(2,1)S(1)} all-to-all(bf16[8,320,1024]{2,1,0:T(8,128)(2,1)S(1)} %copy.52), channel_id=1, replica_groups=mesh['expert'=64,'tensor'=8] {'tensor'}, dimensions={0} | all-to-all | bytes 10485760 | tf_op jit(solution)/shard_map/all_to_all | solution.py:60
  552.7 1.2 convert_reduce_fusion
  553.9 1.8 convolution_convert_fusion.3
  555.6 0.0 copy-done.1
  (5 shorter events, 0.1 us)
Async XLA Ops:
  0.0 234.7 %copy-start = (bf16[1,1024,256]{2,1,0:T(8,128)(2,1)S(1)}, bf16[1,1024,256]{2,1,0:T(8,128)(2,1)}, u32[]{:S(2)}) copy-start(bf16[1,1024,256]{2,1,0:T(8,128)(2,1)} %param.13) | copy-start | bytes 1572868
  220.7 9.7 %copy-start.3 = (bf16[1,1024,256]{2,1,0:T(8,128)(2,1)S(1)}, bf16[1,1024,256]{2,1,0:T(8,128)(2,1)}, u32[]{:S(2)}) copy-start(bf16[1,1024,256]{2,1,0:T(8,128)(2,1)} %param.11) | copy-start | bytes 1572868
  230.4 4.3 copy-start.2
  230.4 6.4 %slice-start = ((s8[5242880]{0:T(1024)(128)(4,1)}), s8[4194304]{0:T(1024)(128)(4,1)S(1)}, s32[]{:S(2)}) async-start(s8[5242880]{0:T(1024)(128)(4,1)} %bitcast.45), calls=%async_computation.4 | async-start | bytes 8388608
  234.7 2.1 slice-start.1
  234.7 2.1 copy-start.4
  484.4 71.2 %copy-start.1 = (bf16[1,1024,256]{2,1,0:T(8,128)(2,1)S(1)}, bf16[1,1024,256]{2,1,0:T(8,128)(2,1)}, u32[]{:S(2)}) copy-start(bf16[1,1024,256]{2,1,0:T(8,128)(2,1)} %param.13) | copy-start | bytes 1572868
